TPU v7x, 32 devices: a whole 2x2x4 slice. The times are simulated.
32 devices in a mesh: cuts: 2 (over y), group: 16 (over z, x, core).
Axes of the slice: x: 2, y: 2, z: 4, core: 2. Of those that a mesh axis runs over, the one named last changes fastest.
Arguments:
- stem_blocks: bfloat16 [2, 64, 1024, 512], P('cuts', None, 'group'), may hold values from -6 to 6
- cap_tensor: bfloat16 [2, 2, 256, 256], P('cuts'), may hold values from -0.1875 to 0.1875
- slot_rows: int32 [64, 1024], P('group'), may hold values from 0 to 1023
- counts: int32 [64], P('group'), may hold values from 128 to 1024, as said below
Outputs:
- amplitudes: bfloat16 [1024, 64, 512], P('cuts', 'group')
Inputs may be any that keep to these rules, and one draw needn't show every extreme that they name: `counts`: some group has exactly 1024 live slots in every draw.
All inputs are finite; a program needn't handle non-finite values.
Results may differ from a plain program's by a relative error of at most 0.0052.
Values may be sent and summed in bfloat16 or wider, within the bound.
No kernel may reach another device: no remote copies, remote signals or barrier semaphores. Data moves between devices by JAX's collectives and lax.ppermute only.
A program may use at most 64 MiB of HBM per device.

v0:
```python
import jax
import jax.numpy as jnp
from jax import lax
from jax.sharding import PartitionSpec as P


def build_matrix(cap_pair):
    real_part = cap_pair[0]
    imag_part = cap_pair[1]
    upper = jnp.concatenate([real_part, imag_part], axis=1)
    lower = jnp.concatenate([-imag_part, real_part], axis=1)
    return jnp.concatenate([upper, lower], axis=0)


def local(stem_blocks, cap_tensor, slot_rows, counts):
    owned_rows = lax.all_to_all(stem_blocks[0], "group", split_axis=0, concat_axis=1, tiled=True)
    matrix = build_matrix(cap_tensor[0])
    slot_total = slot_rows.shape[1]
    share = slot_total // lax.axis_size("cuts")
    positions = jnp.arange(slot_total, dtype=jnp.int32)
    live_mask = positions[None, :] < counts[:, None]
    picked = jnp.take_along_axis(owned_rows, slot_rows[:, :, None], axis=1)
    product = jnp.einsum("gcr,rs->cgs", picked, matrix, preferred_element_type=jnp.float32)
    whole_sum = lax.psum(
        jnp.where(jnp.transpose(live_mask)[:, :, None], product, jnp.float32(0.0)).astype(
            jnp.bfloat16
        ),
        "cuts",
    ).astype(jnp.float32)
    summed = lax.dynamic_slice_in_dim(whole_sum, lax.axis_index("cuts") * share, share, 0)
    return summed.astype(jnp.bfloat16)


def solution(mesh):
    in_specs = (
        P("cuts", None, "group", None),
        P("cuts", None, None, None),
        P("group", None),
        P("group"),
    )
    out_specs = P("cuts", "group", None)
    return jax.shard_map(local, mesh=mesh, in_specs=in_specs, out_specs=out_specs, check_vma=False)
```

profile of v0, /device:TPU:0, one launch (start us, length us, event | category | flops | bytes accessed | tf_op | source)
XLA Modules:
  0.0 309.5 jit_solution(17406738748968861879)
XLA Ops:
  6.5 0.0 copy-start.1
  6.5 0.0 copy-start
  6.5 0.0 copy-start.2
  6.5 7.5 %all-to-all-start = ((bf16[64,64,512]{2,1,0:T(8,128)(2,1)}), bf16[64,64,512]{2,1,0:T(8,128)(2,1)}, u32[]{:S(2)}, u32[]{:S(2)}) async-start(bf16[64,64,512]{2,1,0:T(8,128)(2,1)} %bitcast.29), calls=%async_computation | async-start | bytes 8388608 | tf_op jit(solution)/shard_map/all_to_all | solution.py:16
  14.1 0.0 all-reduce.2.cloned.1.call-start
  14.1 0.0 copy-done.1
  14.2 0.0 copy-done
  14.2 0.1 copy.9
  14.3 0.1 copy.10
  14.4 0.0 copy-done.2
  14.4 0.1 iota_compare_fusion
  14.6 77.2 %all-to-all-done = bf16[64,64,512]{2,1,0:T(8,128)(2,1)} async-done(((bf16[64,64,512]{2,1,0:T(8,128)(2,1)}), bf16[64,64,512]{2,1,0:T(8,128)(2,1)}, u32[]{:S(2)}, u32[]{:S(2)}) %all-to-all-start) | async-done | bytes 4194336 | tf_op jit(solution)/shard_map/all_to_all | solution.py:16
  91.8 4.6 %copy.7 = bf16[16,4,64,512]{3,2,0,1:T(8,128)(2,1)} copy(bf16[16,4,64,512]{3,2,1,0:T(8,128)(2,1)} %bitcast.4) | data formatting | bytes 8388608 | tf_op jit(solution)/shard_map/all_to_all | solution.py:16
  96.4 72.6 %gather_fusion = bf16[4096,512]{1,0:T(8,128)(2,1)} fusion(bf16[4,1024,512]{2,1,0:T(8,128)(2,1)} %bitcast.26, s32[4096]{0:T(1024)S(1)} %bitcast.27), kind=kCustom, calls=%fused_computation | custom fusion | bytes 8421376 | tf_op jit(solution)/shard_map/jit(take_along_axis)/gather | solution.py:22
  169.0 5.8 %fusion = bf16[1024,4,512]{0,2,1:T(8,128)(2,1)} fusion(pred[1024,4]{0,1:T(4,128)(4,1)S(1)} %iota_compare_fusion, bf16[4,1024,512]{2,1,0:T(8,128)(2,1)} %bitcast.28, pred[4,1024]{1,0:T(4,128)(4,1)S(1)} %compare_and_fusion, bf16[256,256]{0,1:T(8,128)(2,1)S(1)} %bitcast.31, bf16[256,256]{0,1:T(8,128)(2,1)S(1)} %bitcast_negate_fusion, ...), kind=kOutput, calls=%fused_computation.2 | convolution fusion | flops 2155872256 | bytes 8790016 | tf_op jit(solution)/shard_map/gcr,rs->cgs/dot_general | solution.py:23
  174.8 0.0 all-reduce.2.cloned.1.call-update
  174.9 123.0 %all-reduce.2.cloned.1.call-done = bf16[1024,4,512]{0,2,1:T(8,128)(2,1)} async-done(((bf16[1024,4,512]{0,2,1:T(8,128)(2,1)}), bf16[1024,4,512]{0,2,1:T(8,128)(2,1)}) %all-reduce.2.cloned.1.call-update) | async-done | bytes 4194320 | tf_op jit(solution)/shard_map/psum | solution.py:24
  297.9 1.7 convert_convert_fusion
  299.6 3.1 copy.8
  (5 shorter events, 0.1 us)
Async XLA Ops:
  6.5 7.6 %copy-start.1 = (s32[4,1024]{1,0:T(4,128)S(1)}, s32[4,1024]{1,0:T(4,128)}, u32[]{:S(2)}) copy-start(s32[4,1024]{1,0:T(4,128)} %param.6) | copy-start | bytes 49156
  6.5 7.6 %copy-start = (bf16[1,2,256,256]{3,2,1,0:T(8,128)(2,1)S(1)}, bf16[1,2,256,256]{3,2,1,0:T(8,128)(2,1)}, u32[]{:S(2)}) copy-start(bf16[1,2,256,256]{3,2,1,0:T(8,128)(2,1)} %param.5) | copy-start | bytes 786436
  6.5 7.9 %copy-start.2 = (s32[4]{0:T(128)S(1)}, s32[4]{0:T(128)}, u32[]{:S(2)}) copy-start(s32[4]{0:T(128)} %param.7) | copy-start | bytes 52
  6.5 85.2 %all-to-all-start = ((bf16[64,64,512]{2,1,0:T(8,128)(2,1)}), bf16[64,64,512]{2,1,0:T(8,128)(2,1)}, u32[]{:S(2)}, u32[]{:S(2)}) async-start(bf16[64,64,512]{2,1,0:T(8,128)(2,1)} %bitcast.29), calls=%async_computation | async-start | bytes 8388608 | tf_op jit(solution)/shard_map/all_to_all | solution.py:16
  14.1 283.8 %all-reduce.2.cloned.1.call-start = ((), (), s32[]{:S(2)}) async-start(), calls=%async_computation.1 | async-start | bytes 8388608 | tf_op jit(solution)/shard_map/psum | solution.py:24
Sparse Core Ops, SparseCore 0:
  175.0 122.8 all-reduce.1
where the time goes:
time: 311 us; the launch traced here: 310 us
  waiting for transfers between devices  200 us (64%)
  local copies, waits for them, and re-layouts  80.5 us (26%)
  between operations  13.5 us (4%)
  starting transfers between devices  7.58 us (2%)
  matrix products  5.84 us (2%)
    psum x1, waiting for transfers between devices, local(): lax.psum(jnp.where(jnp.transpose(live_mask)[:, :, None], product, jnp.flo...  123 us
    all_to_all x1, waiting for transfers between devices, local(): lax.all_to_all(stem_blocks[0], 'group', split_axis=0, concat_axis=1, tile...  77.2 us
    gather x1, local copies, waits for them, and re-layouts, local(): picked = jnp.take_along_axis(owned_rows, slot_rows[:, :, None], axis=1)  72.6 us
    all_to_all x1, starting transfers between devices, local(): lax.all_to_all(stem_blocks[0], 'group', split_axis=0, concat_axis=1, tile...  7.54 us
  transfers between devices with their start and end apart: 2, of which 2 were waited for; matrix products, arithmetic and copies ran while one was open for 0% of the time, Pallas kernels for 0%

commit v1 on v0

--- a/solution.py
+++ b/solution.py
@@ -13,7 +13,11 @@
 
 
 def local(stem_blocks, cap_tensor, slot_rows, counts):
-    owned_rows = lax.all_to_all(stem_blocks[0], "group", split_axis=0, concat_axis=1, tiled=True)
+    base_x = stem_blocks[0]
+    part_next = lax.psum(1, "group")
+    owned_rows = jnp.concatenate(
+        lax.all_to_all(jnp.stack(jnp.split(base_x, part_next, axis=0)), "group", 0, 0), axis=1
+    )
     matrix = build_matrix(cap_tensor[0])
     slot_total = slot_rows.shape[1]
     share = slot_total // lax.axis_size("cuts")

time: 311 us -> 338 us (1.087)
  local copies, waits for them, and re-layouts: 80.5 us -> 107 us
    unnamed x9 -> x24, local copies, waits for them, and re-layouts: 0.21 us -> 25.3 us
    reshape x0 -> x1, local copies, waits for them, and re-layouts: none -> 4.66 us  [local(): jnp.concatenate(lax.all_to_all(jnp.stack(jnp.split(base_x, part_next, axi...]
    all_to_all x1 -> x0, local copies, waits for them, and re-layouts: 4.63 us -> none  [local(): lax.all_to_all(stem_blocks[0], 'group', split_axis=0, concat_axis=1, tile...]
where the time goes in v1:
time: 338 us; the launch traced here: 336 us
  waiting for transfers between devices  200 us (59%)
  local copies, waits for them, and re-layouts  107 us (32%)
  between operations  13.5 us (4%)
  starting transfers between devices  7.58 us (2%)
  matrix products  5.85 us (2%)
    psum x1, waiting for transfers between devices, local(): lax.psum(jnp.where(jnp.transpose(live_mask)[:, :, None], product, jnp.flo...  123 us
    all_to_all x1, waiting for transfers between devices, local(): lax.all_to_all(jnp.stack(jnp.split(base_x, part_next, axis=0)), 'group',...  77.2 us
    gather x1, local copies, waits for them, and re-layouts, local(): picked = jnp.take_along_axis(owned_rows, slot_rows[:, :, None], axis=1)  72.5 us
    unnamed x24, local copies, waits for them, and re-layouts  25.3 us
    all_to_all x1, starting transfers between devices, local(): lax.all_to_all(jnp.stack(jnp.split(base_x, part_next, axis=0)), 'group',...  7.54 us
  transfers between devices with their start and end apart: 2, of which 2 were waited for; matrix products, arithmetic and copies ran while one was open for 0% of the time, Pallas kernels for 0%

profile of v1, /device:TPU:0, one launch (start us, length us, event | category | flops | bytes accessed | tf_op | source)
XLA Modules:
  0.0 336.3 jit_solution(17806805747414089276)
XLA Ops:
  6.5 1.7 slice_dynamic-update-slice_fusion.15
  8.2 1.7 slice_dynamic-update-slice_fusion.14
  9.9 1.7 slice_dynamic-update-slice_fusion.13
  11.6 1.7 slice_dynamic-update-slice_fusion.12
  13.3 1.7 slice_dynamic-update-slice_fusion.11
  15.0 1.7 slice_dynamic-update-slice_fusion.10
  16.6 1.7 slice_dynamic-update-slice_fusion.9
  18.3 1.7 slice_dynamic-update-slice_fusion.8
  20.0 1.7 slice_dynamic-update-slice_fusion.7
  21.6 1.7 slice_dynamic-update-slice_fusion.6
  23.3 1.7 slice_dynamic-update-slice_fusion.5
  25.0 1.7 slice_dynamic-update-slice_fusion.4
  26.6 1.7 slice_dynamic-update-slice_fusion.3
  28.3 1.7 slice_dynamic-update-slice_fusion.2
  30.0 1.7 slice_dynamic-update-slice_fusion.1
  31.6 1.7 slice_dynamic-update-slice_fusion
  33.4 0.0 copy-start.1
  33.4 0.0 copy-start
  33.4 0.0 copy-start.2
  33.4 7.5 %all-to-all-start = ((bf16[16,4,64,512]{3,2,1,0:T(8,128)(2,1)}), bf16[16,4,64,512]{3,2,1,0:T(8,128)(2,1)}, u32[]{:S(2)}, u32[]{:S(2)}) async-start(bf16[16,4,64,512]{3,2,1,0:T(8,128)(2,1)} %slice_dynamic-update-slice_fusion), calls=%async_computation | async-start | bytes 8388608 | tf_op jit(solution)/shard_map/all_to_all | solution.py:19
  40.9 0.0 all-reduce.2.cloned.1.call-start
  41.0 0.0 copy-done.1
  41.0 0.0 copy-done
  41.0 0.1 copy.9
  41.1 0.1 copy.10
  41.3 0.0 copy-done.2
  41.3 0.1 iota_compare_fusion
  41.4 77.2 %all-to-all-done = bf16[16,4,64,512]{3,2,1,0:T(8,128)(2,1)} async-done(((bf16[16,4,64,512]{3,2,1,0:T(8,128)(2,1)}), bf16[16,4,64,512]{3,2,1,0:T(8,128)(2,1)}, u32[]{:S(2)}, u32[]{:S(2)}) %all-to-all-start) | async-done | bytes 4194336 | tf_op jit(solution)/shard_map/all_to_all | solution.py:19
  118.6 4.7 %copy.7 = bf16[4,16,64,512]{3,2,1,0:T(8,128)(2,1)} copy(bf16[4,16,64,512]{3,2,0,1:T(8,128)(2,1)} %bitcast.3) | data formatting | bytes 8388608 | tf_op jit(solution)/shard_map/reshape | solution.py:18
  123.2 72.5 %gather_fusion = bf16[4096,512]{1,0:T(8,128)(2,1)} fusion(bf16[4,1024,512]{2,1,0:T(8,128)(2,1)} %bitcast.23, s32[4096]{0:T(1024)S(1)} %bitcast.24), kind=kCustom, calls=%fused_computation | custom fusion | bytes 8421376 | tf_op jit(solution)/shard_map/jit(take_along_axis)/gather | solution.py:26
  195.7 5.8 %fusion = bf16[1024,4,512]{0,2,1:T(8,128)(2,1)} fusion(pred[1024,4]{0,1:T(4,128)(4,1)S(1)} %iota_compare_fusion, bf16[4,1024,512]{2,1,0:T(8,128)(2,1)} %bitcast.25, pred[4,1024]{1,0:T(4,128)(4,1)S(1)} %compare_and_fusion, bf16[256,256]{0,1:T(8,128)(2,1)S(1)} %bitcast.27, bf16[256,256]{0,1:T(8,128)(2,1)S(1)} %bitcast_negate_fusion, ...), kind=kOutput, calls=%fused_computation.2 | convolution fusion | flops 2155872256 | bytes 8790016 | tf_op jit(solution)/shard_map/gcr,rs->cgs/dot_general | solution.py:27
  201.5 0.0 all-reduce.2.cloned.1.call-update
  201.6 123.0 %all-reduce.2.cloned.1.call-done = bf16[1024,4,512]{0,2,1:T(8,128)(2,1)} async-done(((bf16[1024,4,512]{0,2,1:T(8,128)(2,1)}), bf16[1024,4,512]{0,2,1:T(8,128)(2,1)}) %all-reduce.2.cloned.1.call-update) | async-done | bytes 4194320 | tf_op jit(solution)/shard_map/psum | solution.py:28
  324.6 1.7 convert_convert_fusion
  326.3 3.1 copy.8
  (5 shorter events, 0.1 us)
Async XLA Ops:
  33.4 7.6 %copy-start.1 = (s32[4,1024]{1,0:T(4,128)S(1)}, s32[4,1024]{1,0:T(4,128)}, u32[]{:S(2)}) copy-start(s32[4,1024]{1,0:T(4,128)} %param.6) | copy-start | bytes 49156
  33.4 7.6 %copy-start = (bf16[1,2,256,256]{3,2,1,0:T(8,128)(2,1)S(1)}, bf16[1,2,256,256]{3,2,1,0:T(8,128)(2,1)}, u32[]{:S(2)}) copy-start(bf16[1,2,256,256]{3,2,1,0:T(8,128)(2,1)} %param.5) | copy-start | bytes 786436
  33.4 7.9 %copy-start.2 = (s32[4]{0:T(128)S(1)}, s32[4]{0:T(128)}, u32[]{:S(2)}) copy-start(s32[4]{0:T(128)} %param.7) | copy-start | bytes 52
  33.4 85.2 %all-to-all-start = ((bf16[16,4,64,512]{3,2,1,0:T(8,128)(2,1)}), bf16[16,4,64,512]{3,2,1,0:T(8,128)(2,1)}, u32[]{:S(2)}, u32[]{:S(2)}) async-start(bf16[16,4,64,512]{3,2,1,0:T(8,128)(2,1)} %slice_dynamic-update-slice_fusion), calls=%async_computation | async-start | bytes 8388608 | tf_op jit(solution)/shard_map/all_to_all | solution.py:19
  40.9 283.7 %all-reduce.2.cloned.1.call-start = ((), (), s32[]{:S(2)}) async-start(), calls=%async_computation.1 | async-start | bytes 8388608 | tf_op jit(solution)/shard_map/psum | solution.py:28
Sparse Core Ops, SparseCore 0:
  201.7 122.8 all-reduce.1
